TPU v7x, 512 devices: a whole 4x8x8 slice. The times are simulated.
512 devices in a mesh: row: 8 (over z), col: 16 (over y, core), vox: 4 (over x).
Axes of the slice: x: 4, y: 8, z: 8, core: 2. Of those that a mesh axis runs over, the one named last changes fastest.
Arguments:
- panel_top: bfloat16 [1024, 1024], P('row', ('col', 'vox')), may hold values from -0.059814453 to 0.059814453
- panel_low: bfloat16 [8192, 1024], P('row', ('col', 'vox')), may hold values from -1.1953125 to 1.1953125
- panel_next: bfloat16 [8192, 1024], P('row', ('col', 'vox')), may hold values from -1.1953125 to 1.1953125
- gram_rest: bfloat16 [8192, 8192], P('row', ('col', 'vox')), may hold values from -18 to 18
- inverses: bfloat16 [2, 1024, 1024], P(None, 'row'), as said below
- right_top: bfloat16 [2, 1024, 8192], P(None, None, ('col', 'vox')), may hold values from -1.796875 to 1.796875
- right_low: bfloat16 [8192, 8192], P('row', ('col', 'vox')), may hold values from -24 to 24
Outputs:
- factor: bfloat16 [2, 8192, 1024], P(None, 'row', ('col', 'vox'))
- solved: bfloat16 [2, 1024, 8192], P(None, None, ('col', 'vox'))
- trailing: float32 [8192, 8192], P('row', ('col', 'vox'))
- residual: float32 [8192, 8192], P('row', ('col', 'vox'))
Inputs may be any that keep to these rules, and one draw needn't show every extreme that they name: Each inverses[k] is lower triangular with diagonal entries from 1 to 2.
All inputs are finite; a program needn't handle non-finite values.
Results may differ from a plain program's by a relative error of at most 0.0057.
Values may be sent and summed in bfloat16 or wider, within the bound.
No kernel may reach another device: no remote copies, remote signals or barrier semaphores. Data moves between devices by JAX's collectives and lax.ppermute only.
A program may use at most 64 MiB of HBM per device.

v0:
```python
import jax
import jax.numpy as jnp
from jax import lax
from jax.sharding import PartitionSpec as P


def spread(block, axis, source):
    block = jnp.where(lax.axis_index(axis) == source, block, jnp.zeros_like(block))
    return lax.psum(block, axis)


def contract(left, right):
    return lax.dot_general(
        left, right, (((1,), (1,)), ((), ())), preferred_element_type=jnp.float32
    )


def per_device(panel_top, panel_low, panel_next, gram_rest, inverses, right_top, right_low):
    col_index = lax.axis_index(("col", "vox"))
    row_index = lax.axis_index("row")
    col_width = panel_low.shape[1]
    top_rows = panel_top.shape[0]
    low_rows = panel_low.shape[0]
    rest_cols = gram_rest.shape[1]
    root_row = col_index * rest_cols // low_rows
    whole_inverses = lax.all_gather(inverses, "row", axis=1, tiled=True)
    own_rows = lax.dynamic_slice_in_dim(whole_inverses, col_index * col_width, col_width, 1)
    rows_used = own_rows[0]
    own_top = contract(lax.all_gather(panel_top, ("col", "vox"), axis=1, tiled=True), rows_used)
    own_low = contract(lax.all_gather(panel_low, ("col", "vox"), axis=1, tiled=True), rows_used)
    first_top, first_low = (
        lax.all_gather(own_top.astype(jnp.bfloat16), ("col", "vox"), axis=1, tiled=True),
        lax.all_gather(own_low.astype(jnp.bfloat16), ("col", "vox"), axis=1, tiled=True),
    )
    outgoing = (
        lax.dynamic_slice_in_dim(
            first_top, col_index * col_width - root_row * top_rows, col_width, 0
        ),
        lax.dynamic_slice_in_dim(
            first_low, col_index * rest_cols - root_row * low_rows, rest_cols, 0
        ),
    )
    owner_top, owner_low = (
        spread(outgoing[0], "row", root_row),
        spread(outgoing[1], "row", root_row),
    )
    updated = (panel_next.astype(jnp.float32) - contract(first_low, owner_top)).astype(jnp.bfloat16)
    rows_used = own_rows[1]
    own_next = contract(lax.all_gather(updated, ("col", "vox"), axis=1, tiled=True), rows_used)
    second_low = lax.all_gather(own_next.astype(jnp.bfloat16), ("col", "vox"), axis=1, tiled=True)
    owner_next = spread(
        lax.dynamic_slice_in_dim(
            second_low, col_index * rest_cols - root_row * low_rows, rest_cols, 0
        ),
        "row",
        root_row,
    )
    trailing = (
        gram_rest.astype(jnp.float32)
        - contract(first_low, owner_low)
        - contract(second_low, owner_next)
    )
    first_solve = jnp.dot(
        whole_inverses[0], right_top[0], preferred_element_type=jnp.float32
    ).astype(jnp.bfloat16)
    top_slice = lax.dynamic_slice_in_dim(right_top[1], row_index * top_rows, top_rows, 0)
    top_part = (
        top_slice.astype(jnp.float32)
        - jnp.dot(first_top, first_solve, preferred_element_type=jnp.float32)
    ).astype(jnp.bfloat16)
    top_new = lax.all_gather(top_part, "row", axis=0, tiled=True)
    second_solve = jnp.dot(whole_inverses[1], top_new, preferred_element_type=jnp.float32).astype(
        jnp.bfloat16
    )
    residual = (
        right_low.astype(jnp.float32)
        - jnp.dot(first_low, first_solve, preferred_element_type=jnp.float32)
        - jnp.dot(second_low, second_solve, preferred_element_type=jnp.float32)
    )
    factor = jnp.stack(
        [
            lax.dynamic_slice_in_dim(first_low, col_index * col_width, col_width, 1),
            lax.dynamic_slice_in_dim(second_low, col_index * col_width, col_width, 1),
        ]
    )
    solved = jnp.stack([first_solve, second_solve])
    return (factor, solved, trailing, residual)


def solution(mesh):
    in_specs = (
        P("row", ("col", "vox")),
        P("row", ("col", "vox")),
        P("row", ("col", "vox")),
        P("row", ("col", "vox")),
        P(None, "row", None),
        P(None, None, ("col", "vox")),
        P("row", ("col", "vox")),
    )
    out_specs = (
        P(None, "row", ("col", "vox")),
        P(None, None, ("col", "vox")),
        P("row", ("col", "vox")),
        P("row", ("col", "vox")),
    )
    return jax.shard_map(
        per_device, mesh=mesh, in_specs=in_specs, out_specs=out_specs, check_vma=False
    )
```

profile of v0, /device:TPU:2, one launch (start us, length us, event | category | flops | bytes accessed | tf_op | source)
XLA Modules:
  0.0 587.9 jit_solution(6978349543570293704)
XLA Ops:
  7.2 0.0 copy-start.7
  7.2 0.0 all-gather.8.cloned.1.call-start
  7.2 0.7 all-gather.8.cloned.1.call-update
  7.9 0.0 all-gather.6.cloned.1.call-start
  8.0 0.7 all-gather.6.cloned.1.call-update
  8.7 0.0 copy-start.6
  8.7 0.0 all-gather.10.cloned.1.call-start
  8.7 88.6 %all-gather.8.cloned.1.call-done = bf16[1024,1024]{0,1:T(8,128)(2,1)} async-done(((bf16[1024,16]{0,1:T(8,128)(2,1)}), bf16[1024,1024]{0,1:T(8,128)(2,1)}) %all-gather.8.cloned.1.call-update) | async-done | bytes 2097168 | tf_op jit(solution)/shard_map/all_gather | solution.py:30
  97.4 59.5 %all-gather.6.cloned.1.call-done = bf16[2,1024,1024]{2,1,0:T(8,128)(2,1)} async-done(((bf16[2,128,1024]{2,1,0:T(8,128)(2,1)}), bf16[2,1024,1024]{2,1,0:T(8,128)(2,1)}) %all-gather.6.cloned.1.call-update) | async-done | bytes 4194320 | tf_op jit(solution)/shard_map/all_gather | solution.py:26
  156.9 2.6 fusion.6
  159.5 0.0 all-gather.10.cloned.1.call-update
  159.5 0.0 all-gather.12.cloned.1.call-start
  159.6 0.0 copy-done.7
  159.6 69.7 %all_gather.27 = bf16[128,1024]{0,1:T(8,128)(2,1)S(1)} all-gather(bf16[128,16]{0,1:T(8,128)(2,1)S(1)} %copy-done.7), channel_id=1, replica_groups=mesh['row'=8,'col'=16,'vox'=4] {'col','vox'}, dimensions={1}, use_global_device_ids=true | all-gather | bytes 266240 | tf_op jit(solution)/shard_map/all_gather | solution.py:29
  229.3 0.9 fusion.7
  230.2 66.4 %all_gather.28 = bf16[128,1024]{0,1:T(8,128)(2,1)S(1)} all-gather(bf16[128,16]{0,1:T(8,128)(2,1)S(1)} %fusion.7), channel_id=1, replica_groups=mesh['row'=8,'col'=16,'vox'=4] {'col','vox'}, dimensions={1}, use_global_device_ids=true | all-gather | bytes 266240 | tf_op jit(solution)/shard_map/all_gather | solution.py:32
  296.6 0.1 dynamic-slice_select_fusion.2
  296.8 31.6 %psum.21 = bf16[16,1024]{0,1:T(8,128)(2,1)S(1)} all-reduce(bf16[16,1024]{0,1:T(8,128)(2,1)S(1)} %dynamic-slice_select_fusion.2), channel_id=1, replica_groups=mesh['row'=8,'col'=16,'vox'=4] {'row'}, use_global_device_ids=true, to_apply=%region_0.1 | all-reduce | flops 16384 | bytes 65536 | tf_op jit(solution)/shard_map/psum | solution.py:9
  328.3 0.0 copy-start.4
  328.4 0.0 all-gather.10.cloned.1.call-done
  328.4 0.0 copy-done.6
  328.4 2.7 fusion.4
  331.1 0.0 all-gather.12.cloned.1.call-update
  331.1 0.0 all-gather.14.cloned.1.call-start
  331.2 80.5 %all-gather.12.cloned.1.call-done = bf16[1024,1024]{0,1:T(8,128)(2,1)} async-done(((bf16[1024,16]{0,1:T(8,128)(2,1)}), bf16[1024,1024]{0,1:T(8,128)(2,1)}) %all-gather.12.cloned.1.call-update) | async-done | bytes 2097168 | tf_op jit(solution)/shard_map/all_gather | solution.py:49
  411.7 2.6 convolution_convert_fusion
  414.3 0.0 all-gather.14.cloned.1.call-update
  414.3 0.0 all-reduce.3.cloned.1.call-start
  414.4 0.0 slice-start
  414.4 0.0 copy-done.4
  414.4 0.0 copy-start.8
  414.4 2.4 fusion.2
  416.9 0.0 slice-done
  416.9 0.3 fusion.5
  417.2 26.8 %all_gather.31 = bf16[1024,128]{1,0:T(8,128)(2,1)S(1)} all-gather(bf16[128,128]{1,0:T(8,128)(2,1)S(1)} %fusion.5), channel_id=1, replica_groups=mesh['row'=8,'col'=16,'vox'=4] {'row'}, dimensions={0}, use_global_device_ids=true | all-gather | bytes 294912 | tf_op jit(solution)/shard_map/all_gather | solution.py:71
  444.0 0.0 copy-done.8
  444.0 0.0 copy-start
  444.0 0.0 copy-start.2
  444.0 0.7 fusion.3
  444.7 0.8 pad_maximum_fusion
  445.5 0.0 copy-done
  445.6 0.8 dynamic-slice_select_fusion.1
  446.3 0.0 copy-done.2
  446.3 0.7 convolution_subtract_fusion.1
  447.1 48.9 %all-gather.14.cloned.1.call-done = bf16[1024,1024]{0,1:T(8,128)(2,1)} async-done(((bf16[1024,16]{0,1:T(8,128)(2,1)}), bf16[1024,1024]{0,1:T(8,128)(2,1)}) %all-gather.14.cloned.1.call-update) | async-done | bytes 2097168 | tf_op jit(solution)/shard_map/all_gather | solution.py:50
  496.0 1.7 dynamic-slice_select_fusion
  497.7 0.0 all-reduce.3.cloned.1.call-update
  497.7 0.8 dynamic-slice_bitcast_fusion.3
  498.4 0.6 pad_maximum_fusion.1
  499.1 0.0 copy-start.3
  499.1 3.2 convolution_subtract_fusion
  502.3 75.4 %all-reduce.3.cloned.1.call-done = (bf16[128,1024]{0,1:T(8,128)(2,1)}, bf16[128,1024]{0,1:T(8,128)(2,1)}) async-done(((bf16[128,1024]{0,1:T(8,128)(2,1)}, bf16[128,1024]{0,1:T(8,128)(2,1)}), (bf16[128,1024]{0,1:T(8,128)(2,1)}, bf16[128,1024]{0,1:T(8,128)(2,1)})) %all-reduce.3.cloned.1.call-update) | async-done | bytes 524304 | tf_op jit(solution)/shard_map/psum | solution.py:9
  577.6 0.0 copy-done.3
  577.6 0.0 copy-start.1
  577.6 0.0 copy-start.5
  577.6 1.8 convolution_subtract_fusion.3
  579.5 0.0 copy-done.1
  579.5 0.0 copy-done.5
  579.5 1.5 convolution_subtract_fusion.2
  (1 shorter events, 0.0 us)
Async XLA Ops:
  7.2 152.4 %copy-start.7 = (bf16[128,16]{0,1:T(8,128)(2,1)S(1)}, bf16[128,16]{0,1:T(8,128)(2,1)}, u32[]{:S(2)}) copy-start(bf16[128,16]{0,1:T(8,128)(2,1)} %param.7) | copy-start | bytes 12292
  7.2 90.2 %all-gather.8.cloned.1.call-start = ((), (), s32[]{:S(2)}) async-start(), calls=%async_computation.1 | async-start | bytes 2129920 | tf_op jit(solution)/shard_map/all_gather | solution.py:30
  7.9 149.0 %all-gather.6.cloned.1.call-start = ((), (), s32[]{:S(2)}) async-start(), calls=%async_computation | async-start | bytes 4718592 | tf_op jit(solution)/shard_map/all_gather | solution.py:26
  8.7 319.7 %copy-start.6 = (bf16[1024,16]{0,1:T(8,128)(2,1)S(1)}, bf16[1024,16]{0,1:T(8,128)(2,1)}, u32[]{:S(2)}) copy-start(bf16[1024,16]{0,1:T(8,128)(2,1)} %param.9) | copy-start | bytes 98308
  8.7 319.7 %all-gather.10.cloned.1.call-start = ((), (), s32[]{:S(2)}) async-start(), calls=%async_computation.2 | async-start | bytes 2129920 | tf_op jit(solution)/shard_map/all_gather | solution.py:33
  159.5 252.2 %all-gather.12.cloned.1.call-start = ((), (), s32[]{:S(2)}) async-start(), calls=%async_computation.3 | async-start | bytes 2129920 | tf_op jit(solution)/shard_map/all_gather | solution.py:49
  328.3 86.1 %copy-start.4 = (bf16[2,1024,128]{2,1,0:T(8,128)(2,1)S(1)}, bf16[2,1024,128]{2,1,0:T(8,128)(2,1)}, u32[]{:S(2)}) copy-start(bf16[2,1024,128]{2,1,0:T(8,128)(2,1)} %param.12) | copy-start | bytes 1572868
  331.1 164.9 %all-gather.14.cloned.1.call-start = ((), (), s32[]{:S(2)}) async-start(), calls=%async_computation.4 | async-start | bytes 2129920 | tf_op jit(solution)/shard_map/all_gather | solution.py:50
  414.3 163.3 %all-reduce.3.cloned.1.call-start = ((), (), s32[]{:S(2)}) async-start(), calls=%async_computation.5 | async-start | bytes 1048576 | tf_op jit(solution)/shard_map/psum | solution.py:9
  414.4 2.5 slice-start
  414.4 29.5 %copy-start.8 = (bf16[2,1024,1024]{2,1,0:T(8,128)(2,1)S(1)}, bf16[2,1024,1024]{2,1,0:T(8,128)(2,1)}, u32[]{:S(2)}) copy-start(bf16[2,1024,1024]{2,1,0:T(8,128)(2,1)} %all-gather.6.cloned.1.call-done) | copy-start | bytes 12582916
  444.0 1.6 copy-start
  444.0 2.4 copy-start.2
  499.1 78.6 %copy-start.3 = (bf16[1024,128]{1,0:T(8,128)(2,1)S(1)}, bf16[1024,128]{1,0:T(8,128)(2,1)}, u32[]{:S(2)}) copy-start(bf16[1024,128]{1,0:T(8,128)(2,1)} %param.10) | copy-start | bytes 786436
  577.6 1.8 copy-start.1
  577.6 1.9 copy-start.5
Sparse Core Ops, SparseCore 0:
  11.4 85.9 all-gather.7
  99.5 57.3 all-gather.5
  160.8 79.4 all-gather.9
  331.2 80.4 all-gather.11
  415.5 80.4 all-gather.13
  498.8 78.8 all-reduce.2
where the time goes:
time: 588 us
  waiting for transfers between devices  354 us (60%)
  blocking collectives  194 us (33%)
  matrix products  19.5 us (3%)
  between operations  14.3 us (2%)
    all_gather x1, waiting for transfers between devices, per_device(): lax.all_gather(panel_low, ('col', 'vox'), axis=1, tiled=True)  88.6 us
    all_gather x1, waiting for transfers between devices, per_device(): lax.all_gather(updated, ('col', 'vox'), axis=1, tiled=True)  80.5 us
    psum x1, waiting for transfers between devices, spread(): return lax.psum(block, axis)  75.4 us
    all_gather x1, blocking collectives, per_device(): lax.all_gather(panel_top, ('col', 'vox'), axis=1, tiled=True)  69.7 us
    all_gather x1, blocking collectives, per_device(): lax.all_gather(own_top.astype(jnp.bfloat16), ('col', 'vox'), axis=1, tile...  66.4 us
    all_gather x1, waiting for transfers between devices, per_device(): whole_inverses = lax.all_gather(inverses, 'row', axis=1, tiled=True)  59.5 us
    all_gather x1, waiting for transfers between devices, per_device(): lax.all_gather(own_next.astype(jnp.bfloat16), ('col', 'vox'), axis=1, til...  48.9 us
    psum x1, blocking collectives, spread(): return lax.psum(block, axis)  31.6 us
  transfers between devices with their start and end apart: 6, of which 5 were waited for; matrix products, arithmetic and copies ran while one was open for 2% of the time, Pallas kernels for 0%

commit v1 on v0

--- a/solution.py
+++ b/solution.py
@@ -6,7 +6,7 @@
 
 def spread(block, axis, source):
     block = jnp.where(lax.axis_index(axis) == source, block, jnp.zeros_like(block))
-    return lax.psum(block, axis)
+    return jnp.sum(lax.all_gather(block, axis), axis=0)
 
 
 def contract(left, right):

time: 588 us -> 606 us (1.031)
  waiting for transfers between devices: 354 us -> 373 us
    psum x1 -> x0, waiting for transfers between devices: 75.4 us -> none  [spread(): return lax.psum(block, axis)]
    all_gather x0 -> x2, waiting for transfers between devices: none -> 62.8 us  [spread(): return jnp.sum(lax.all_gather(block, axis), axis=0)]
    all_gather x1, waiting for transfers between devices: 48.9 us -> 80.7 us  [per_device(): lax.all_gather(own_next.astype(jnp.bfloat16), ('col', 'vox'), axis=1, til...]
    psum x1 -> x0, blocking collectives: 31.6 us -> none  [spread(): return lax.psum(block, axis)]
    all_gather x0 -> x1, blocking collectives: none -> 24.9 us  [spread(): return jnp.sum(lax.all_gather(block, axis), axis=0)]
  transfers between devices with their start and end apart: 6 -> 7, of which waited for: 5 -> 6; matrix products, arithmetic and copies ran while one was open for 2% -> 3% of each run, Pallas kernels for 0% -> 0%
where the time goes in v1:
time: 606 us; the launch traced here: 605 us
  waiting for transfers between devices  373 us (62%)
  blocking collectives  188 us (31%)
  matrix products  16.9 us (3%)
  between operations  14.4 us (2%)
  other arithmetic  7.22 us (1%)
    all_gather x1, waiting for transfers between devices, per_device(): lax.all_gather(panel_low, ('col', 'vox'), axis=1, tiled=True)  88.6 us
    all_gather x1, waiting for transfers between devices, per_device(): lax.all_gather(own_next.astype(jnp.bfloat16), ('col', 'vox'), axis=1, til...  80.7 us
    all_gather x1, waiting for transfers between devices, per_device(): lax.all_gather(updated, ('col', 'vox'), axis=1, tiled=True)  79.7 us
    all_gather x1, blocking collectives, per_device(): lax.all_gather(panel_top, ('col', 'vox'), axis=1, tiled=True)  69.7 us
    all_gather x1, blocking collectives, per_device(): lax.all_gather(own_top.astype(jnp.bfloat16), ('col', 'vox'), axis=1, tile...  66.4 us
    all_gather x2, waiting for transfers between devices, spread(): return jnp.sum(lax.all_gather(block, axis), axis=0)  62.8 us
    all_gather x1, waiting for transfers between devices, per_device(): whole_inverses = lax.all_gather(inverses, 'row', axis=1, tiled=True)  59.5 us
    all_gather x1, blocking collectives, per_device(): top_new = lax.all_gather(top_part, 'row', axis=0, tiled=True)  27.3 us
  transfers between devices with their start and end apart: 7, of which 6 were waited for; matrix products, arithmetic and copies ran while one was open for 3% of the time, Pallas kernels for 0%

profile of v1, /device:TPU:2, one launch (start us, length us, event | category | flops | bytes accessed | tf_op | source)
XLA Modules:
  0.0 605.3 jit_solution(7562011301278253595)
XLA Ops:
  7.2 0.0 copy-start.7
  7.2 0.0 all-gather.13.cloned.1.call-start
  7.2 0.7 all-gather.13.cloned.1.call-update
  7.9 0.0 all-gather.11.cloned.1.call-start
  8.0 0.7 all-gather.11.cloned.1.call-update
  8.7 0.0 all-gather.15.cloned.1.call-start
  8.7 0.0 copy-start.6
  8.7 88.6 %all-gather.13.cloned.1.call-done = bf16[1024,1024]{0,1:T(8,128)(2,1)} async-done(((bf16[1024,16]{0,1:T(8,128)(2,1)}), bf16[1024,1024]{0,1:T(8,128)(2,1)}) %all-gather.13.cloned.1.call-update) | async-done | bytes 2097168 | tf_op jit(solution)/shard_map/all_gather | solution.py:30
  97.4 59.5 %all-gather.11.cloned.1.call-done = bf16[2,1024,1024]{2,1,0:T(8,128)(2,1)} async-done(((bf16[2,128,1024]{2,1,0:T(8,128)(2,1)}), bf16[2,1024,1024]{2,1,0:T(8,128)(2,1)}) %all-gather.11.cloned.1.call-update) | async-done | bytes 4194320 | tf_op jit(solution)/shard_map/all_gather | solution.py:26
  156.9 2.6 fusion.6
  159.5 0.0 all-gather.15.cloned.1.call-update
  159.5 0.0 all-gather.17.cloned.1.call-start
  159.6 0.0 copy-done.7
  159.6 69.7 %all_gather.45 = bf16[128,1024]{0,1:T(8,128)(2,1)S(1)} all-gather(bf16[128,16]{0,1:T(8,128)(2,1)S(1)} %copy-done.7), channel_id=1, replica_groups=mesh['row'=8,'col'=16,'vox'=4] {'col','vox'}, dimensions={1}, use_global_device_ids=true | all-gather | bytes 266240 | tf_op jit(solution)/shard_map/all_gather | solution.py:29
  229.3 0.9 fusion.7
  230.2 66.4 %all_gather.46 = bf16[128,1024]{0,1:T(8,128)(2,1)S(1)} all-gather(bf16[128,16]{0,1:T(8,128)(2,1)S(1)} %fusion.7), channel_id=1, replica_groups=mesh['row'=8,'col'=16,'vox'=4] {'col','vox'}, dimensions={1}, use_global_device_ids=true | all-gather | bytes 266240 | tf_op jit(solution)/shard_map/all_gather | solution.py:32
  296.6 0.1 dynamic-slice_select_fusion.2
  296.8 0.1 copy.14
  296.9 24.9 %all-gather = bf16[128,1024]{1,0:T(8,128)(2,1)S(1)} all-gather(bf16[16,1024]{1,0:T(8,128)(2,1)S(1)} %copy.14), channel_id=2, replica_groups=mesh['row'=8,'col'=16,'vox'=4] {'row'}, dimensions={0}, use_global_device_ids=true | all-gather | bytes 294912 | tf_op jit(solution)/shard_map/all_gather | solution.py:9
  321.8 0.0 all-gather.15.cloned.1.call-done
  321.9 0.0 copy-done.6
  321.9 0.0 copy-start
  321.9 2.7 fusion.4
  324.6 0.0 all-gather.17.cloned.1.call-update
  324.7 0.0 all-gather.19.cloned.1.call-start
  324.7 0.0 copy-start.5
  324.7 79.7 %all-gather.17.cloned.1.call-done = bf16[1024,1024]{0,1:T(8,128)(2,1)} async-done(((bf16[1024,16]{0,1:T(8,128)(2,1)}), bf16[1024,1024]{0,1:T(8,128)(2,1)}) %all-gather.17.cloned.1.call-update) | async-done | bytes 2097168 | tf_op jit(solution)/shard_map/all_gather | solution.py:49
  404.5 2.6 convolution_convert_fusion
  407.1 0.0 all-gather.19.cloned.1.call-update
  407.1 0.0 all-gather.21.cloned.1.call-start
  407.2 0.0 copy-done
  407.2 0.8 dynamic-slice_select_fusion.1
  407.9 0.0 all-gather.21.cloned.1.call-update
  408.0 0.0 all-gather.23.cloned.1.call-start
  408.0 80.7 %all-gather.19.cloned.1.call-done = bf16[1024,1024]{0,1:T(8,128)(2,1)} async-done(((bf16[1024,16]{0,1:T(8,128)(2,1)}), bf16[1024,1024]{0,1:T(8,128)(2,1)}) %all-gather.19.cloned.1.call-update) | async-done | bytes 2097168 | tf_op jit(solution)/shard_map/all_gather | solution.py:50
  488.7 1.7 dynamic-slice_select_fusion
  490.4 0.0 all-gather.23.cloned.1.call-update
  490.4 0.0 slice-start
  490.5 0.0 copy-done.5
  490.5 0.0 copy-start.8
  490.5 2.4 fusion.2
  492.9 0.0 slice-done
  492.9 0.3 fusion.5
  493.2 27.3 %all_gather.51 = bf16[1024,128]{1,0:T(8,128)(2,1)S(1)} all-gather(bf16[128,128]{1,0:T(8,128)(2,1)S(1)} %fusion.5), channel_id=1, replica_groups=mesh['row'=8,'col'=16,'vox'=4] {'row'}, dimensions={0}, use_global_device_ids=true | all-gather | bytes 294912 | tf_op jit(solution)/shard_map/all_gather | solution.py:71
  520.5 0.7 fusion.3
  521.2 0.8 pad_maximum_fusion
  522.0 0.0 copy-done.3
  522.0 0.7 convolution_subtract_fusion.1
  522.8 20.0 %all-gather.21.cloned.1.call-done = bf16[1024,1024]{0,1:T(8,128)(2,1)} async-done(((bf16[128,1024]{0,1:T(8,128)(2,1)}), bf16[1024,1024]{0,1:T(8,128)(2,1)}) %all-gather.21.cloned.1.call-update) | async-done | bytes 2097168 | tf_op jit(solution)/shard_map/all_gather | solution.py:9
  542.8 2.2 copy.17
  545.0 0.0 copy-start.4
  545.0 1.5 bitcast_reduce_fusion.1
  546.6 0.0 copy-done.4
  546.6 0.0 copy-start.1
  546.6 0.7 convolution_subtract_fusion.3
  547.3 0.8 copy-done.1
  548.2 0.6 pad_maximum_fusion.1
  548.8 1.5 convolution_subtract_fusion
  550.3 42.8 %all-gather.23.cloned.1.call-done = bf16[1024,1024]{0,1:T(8,128)(2,1)} async-done(((bf16[128,1024]{0,1:T(8,128)(2,1)}), bf16[1024,1024]{0,1:T(8,128)(2,1)}) %all-gather.23.cloned.1.call-update) | async-done | bytes 2097168 | tf_op jit(solution)/shard_map/all_gather | solution.py:9
  593.1 2.2 copy.18
  595.3 0.0 copy-start.2
  595.3 1.5 bitcast_reduce_fusion
  596.9 0.0 copy-done.2
  596.9 1.5 convolution_subtract_fusion.2
  (5 shorter events, 0.1 us)
Async XLA Ops:
  7.2 152.4 %copy-start.7 = (bf16[128,16]{0,1:T(8,128)(2,1)S(1)}, bf16[128,16]{0,1:T(8,128)(2,1)}, u32[]{:S(2)}) copy-start(bf16[128,16]{0,1:T(8,128)(2,1)} %param.7) | copy-start | bytes 12292
  7.2 90.2 %all-gather.13.cloned.1.call-start = ((), (), s32[]{:S(2)}) async-start(), calls=%async_computation.1 | async-start | bytes 2129920 | tf_op jit(solution)/shard_map/all_gather | solution.py:30
  7.9 149.0 %all-gather.11.cloned.1.call-start = ((), (), s32[]{:S(2)}) async-start(), calls=%async_computation | async-start | bytes 4718592 | tf_op jit(solution)/shard_map/all_gather | solution.py:26
  8.7 313.2 %all-gather.15.cloned.1.call-start = ((), (), s32[]{:S(2)}) async-start(), calls=%async_computation.2 | async-start | bytes 2129920 | tf_op jit(solution)/shard_map/all_gather | solution.py:33
  8.7 313.2 %copy-start.6 = (bf16[1024,16]{0,1:T(8,128)(2,1)S(1)}, bf16[1024,16]{0,1:T(8,128)(2,1)}, u32[]{:S(2)}) copy-start(bf16[1024,16]{0,1:T(8,128)(2,1)} %param.9) | copy-start | bytes 98308
  159.5 245.0 %all-gather.17.cloned.1.call-start = ((), (), s32[]{:S(2)}) async-start(), calls=%async_computation.3 | async-start | bytes 2129920 | tf_op jit(solution)/shard_map/all_gather | solution.py:49
  321.9 85.3 %copy-start = (bf16[1024,1024]{0,1:T(8,128)(2,1)S(1)}, bf16[1024,1024]{0,1:T(8,128)(2,1)}, u32[]{:S(2)}) copy-start(bf16[1024,1024]{0,1:T(8,128)(2,1)} %all-gather.15.cloned.1.call-done) | copy-start | bytes 6291460
  324.7 164.1 %all-gather.19.cloned.1.call-start = ((), (), s32[]{:S(2)}) async-start(), calls=%async_computation.4 | async-start | bytes 2129920 | tf_op jit(solution)/shard_map/all_gather | solution.py:50
  324.7 165.8 %copy-start.5 = (bf16[2,1024,128]{2,1,0:T(8,128)(2,1)S(1)}, bf16[2,1024,128]{2,1,0:T(8,128)(2,1)}, u32[]{:S(2)}) copy-start(bf16[2,1024,128]{2,1,0:T(8,128)(2,1)} %param.12) | copy-start | bytes 1572868
  407.1 135.7 %all-gather.21.cloned.1.call-start = ((), (), s32[]{:S(2)}) async-start(), calls=%async_computation.5 | async-start | bytes 2359296 | tf_op jit(solution)/shard_map/all_gather | solution.py:9
  408.0 185.1 %all-gather.23.cloned.1.call-start = ((), (), s32[]{:S(2)}) async-start(), calls=%async_computation.6 | async-start | bytes 2359296 | tf_op jit(solution)/shard_map/all_gather | solution.py:9
  490.4 2.5 slice-start
  490.5 30.0 %copy-start.8 = (bf16[2,1024,1024]{2,1,0:T(8,128)(2,1)S(1)}, bf16[2,1024,1024]{2,1,0:T(8,128)(2,1)}, u32[]{:S(2)}) copy-start(bf16[2,1024,1024]{2,1,0:T(8,128)(2,1)} %all-gather.11.cloned.1.call-done) | copy-start | bytes 12582916
  520.5 1.6 copy-start.3
  545.0 1.6 copy-start.4
  546.6 1.6 copy-start.1
  595.3 1.6 copy-start.2
Sparse Core Ops, SparseCore 0:
  11.4 85.9 all-gather.12
  99.5 57.3 all-gather.10
  160.8 79.4 all-gather.14
  324.8 79.6 all-gather.16
  408.2 80.4 all-gather.18
  491.1 51.5 all-gather.20
  545.4 47.6 all-gather.22
